TPU v7x, 32 devices: a whole 2x2x4 slice. The times are simulated.
32 devices in a mesh: blk: 4 (over y, core), group: 8 (over z, x).
Axes of the slice: x: 2, y: 2, z: 4, core: 2. Of those that a mesh axis runs over, the one named last changes fastest.
Arguments:
- queries: bfloat16 [32, 16, 128], P(('blk', 'group')), may hold values from -2.5 to 2.5
- query_mask: int32 [32, 16], P(('blk', 'group')), may hold values from 0 to 1, as said below
- positive: int32 [32], P(('blk', 'group')), may hold values from 0 to 63
- page_vectors: bfloat16 [64, 128, 128], P(('blk', 'group')), may hold values from -2 to 2
- page_mask: int32 [64, 128], P(('blk', 'group')), may hold values from 0 to 1, as said below
Outputs:
- grad_queries: float32 [32, 16, 128], P(('blk', 'group'))
- grad_pages: float32 [64, 128, 128], P(('blk', 'group'))
- mean_loss: float32 [], replicated
Inputs may be any that keep to these rules, and one draw needn't show every extreme that they name: `query_mask`: each row holds ones on its first 8 to 16 token slots and zeros after them. `page_mask`: each row holds ones on its first 32 to 128 patch slots and zeros after them.
All inputs are finite; a program needn't handle non-finite values.
Results may differ from a plain program's by a relative error of at most 0.0028.
Values may be sent and summed in bfloat16 or wider, within the bound.
No kernel may reach another device: no remote copies, remote signals or barrier semaphores. Data moves between devices by JAX's collectives and lax.ppermute only.
A program may use at most 64 MiB of HBM per device.

v0:
```python
import math
import jax
import jax.numpy as jnp
from jax import lax
from jax.sharding import PartitionSpec as P

relaxation_scale_factor = 0.5
guarded_floor_entry = -1e30


def combined_all(part, axis, combine):
    gathered = jax.tree.map(lambda a: lax.all_gather(a, axis), part)

    def take(source):
        return jax.tree.map(lambda a: lax.dynamic_index_in_dim(a, source, 0, False), gathered)

    return lax.fori_loop(
        1, lax.axis_size(axis), lambda source, state: combine(state, take(source)), take(0)
    )


def from_behind(value, axis, steps):
    count = lax.axis_size(axis)
    pairs = [(source, (source + steps) % count) for source in range(count)]
    return lax.ppermute(value, axis, pairs)


def masked_logits(row_block, lone_document, live_image_embeddings):
    similarity_matrix = lax.dot_general(
        row_block, lone_document, (((1,), (1,)), ((), ())), preferred_element_type=jnp.float32
    )
    return jnp.where(
        live_image_embeddings[None, :] > 0,
        similarity_matrix / relaxation_scale_factor,
        guarded_floor_entry,
    )


def combine_parts(earlier, later):
    highest = jnp.maximum(earlier[0], later[0])
    totals = earlier[1] * jnp.exp(earlier[0] - highest) + later[1] * jnp.exp(later[0] - highest)
    return (highest, totals, earlier[2] + later[2])


def on_device(queries, query_mask, positive, page_vectors, page_mask):
    tokens = queries.shape[1]
    features = queries.shape[2]
    local_pages = page_vectors.shape[0]
    blocks = lax.axis_size("blk")
    members = lax.axis_size("group")
    bundle_size = queries.shape[0] * members
    total_queries = bundle_size * blocks
    natural_logarithm_lengths = jnp.log(jnp.sum(page_mask.astype(jnp.float32), axis=1))
    bundle_vectors, bundle_masks, bundle_targets = (
        lax.all_gather(queries, "group", axis=0, tiled=True),
        lax.all_gather(query_mask, "group", axis=0, tiled=True),
        lax.all_gather(positive, "group", axis=0, tiled=True),
    )

    def forward_piece(folded, shard_in, root_row):
        scores, lse_rows, live_all, owners, kept = folded
        vectors, token_masks, targets = shard_in
        amount = vectors.shape[0]
        stride = math.gcd(amount, max(1, 512 // tokens))

        def run_block(number, current):
            scores, lse_rows = current
            offset = number * stride
            slab_rows = lax.dynamic_slice_in_dim(vectors, offset, stride, 0).reshape(
                stride * tokens, features
            )
            alive = lax.dynamic_slice_in_dim(token_masks, offset, stride, 0).astype(jnp.float32)
            found_sums = []
            for index_page in range(local_pages):
                masked = masked_logits(slab_rows, page_vectors[index_page], page_mask[index_page])
                highest = jnp.max(masked, axis=1, keepdims=True)
                found_sums.append(
                    highest[:, 0] + jnp.log(jnp.sum(jnp.exp(masked - highest), axis=1))
                )
            logsumexp_results = jnp.stack(found_sums, axis=1).reshape(stride, tokens, local_pages)
            softened_supremum = relaxation_scale_factor * (
                logsumexp_results - natural_logarithm_lengths
            )
            page_score = jnp.sum(alive[:, :, None] * softened_supremum, axis=1)
            scores = lax.dynamic_update_slice_in_dim(scores, page_score, offset, 0)
            lse_rows = lax.dynamic_update_slice_in_dim(lse_rows, logsumexp_results, offset, 0)
            return (scores, lse_rows)

        scores, lse_rows = lax.fori_loop(0, amount // stride, run_block, (scores, lse_rows))
        live_all = lax.dynamic_update_slice_in_dim(live_all, token_masks, root_row, 0)
        owners = lax.dynamic_update_slice_in_dim(owners, targets, root_row, 0)
        kept = vectors
        return (scores, lse_rows, live_all, owners, kept)

    starting = (
        jnp.zeros((total_queries, local_pages), jnp.float32),
        jnp.zeros((total_queries, tokens, local_pages), jnp.float32),
        jnp.zeros((total_queries, tokens), jnp.int32),
        jnp.zeros((total_queries,), jnp.int32),
        jnp.zeros((total_queries, tokens, features), jnp.bfloat16),
    )
    scores, lse_rows, live_all, owners, kept = forward_piece(
        starting,
        (
            lax.all_gather(bundle_vectors, "blk", axis=0, tiled=True),
            lax.all_gather(bundle_masks, "blk", axis=0, tiled=True),
            lax.all_gather(bundle_targets, "blk", axis=0, tiled=True),
        ),
        jnp.int32(0),
    )
    position = lax.axis_index(("blk", "group"))
    page_ids = position * local_pages + jnp.arange(local_pages, dtype=jnp.int32)
    chosen = owners[:, None] == page_ids[None, :]
    picked_local = jnp.sum(jnp.where(chosen, scores, 0.0))
    local_top = jnp.max(scores, axis=1)
    local_total = jnp.sum(jnp.exp(scores - local_top[:, None]), axis=1)
    highest, totals, picked = combined_all(
        (local_top, local_total, picked_local), ("blk", "group"), combine_parts
    )
    page_lse = highest + jnp.log(totals)
    mean_loss = (jnp.sum(page_lse) - picked) / total_queries
    coefficient = jnp.exp(scores - page_lse[:, None]) - chosen.astype(jnp.float32)
    factor_scale = coefficient[:, None, :] * live_all.astype(jnp.float32)[:, :, None]

    def slice_rows(root_row, amount):
        sums = lax.dynamic_slice_in_dim(lse_rows, root_row, amount, 0).reshape(
            amount * tokens, local_pages
        )
        scales = lax.dynamic_slice_in_dim(factor_scale, root_row, amount, 0).reshape(
            amount * tokens, local_pages
        )
        return (sums, scales)

    def gradient_terms(row_block, logsumexp_results, scales, page_grads):
        partial_value = jnp.zeros(row_block.shape, jnp.float32)
        for number in range(local_pages):
            masked = masked_logits(row_block, page_vectors[number], page_mask[number])
            weights = jnp.exp(masked - logsumexp_results[:, number : number + 1])
            factor = (scales[:, number : number + 1] * weights).astype(jnp.bfloat16)
            partial_value = partial_value + jnp.dot(
                factor, page_vectors[number], preferred_element_type=jnp.float32
            )
            update = lax.dot_general(
                factor, row_block, (((0,), (0,)), ((), ())), preferred_element_type=jnp.float32
            )
            page_grads = page_grads.at[number].add(update)
        return (partial_value, page_grads)

    home = lax.axis_index("blk")
    page_grads = jnp.zeros(page_vectors.shape, jnp.float32)

    def visit_one(moving, collected, page_grads, lap_index):
        root_row = (home - lap_index) % blocks * bundle_size
        sums, scales = slice_rows(root_row, bundle_size)
        partial_value, page_grads = gradient_terms(
            moving.reshape(bundle_size * tokens, features), sums, scales, page_grads
        )
        return (collected + partial_value.reshape(bundle_size, tokens, features), page_grads)

    def pass_one(collected):
        return from_behind(collected, "blk", 1)

    def turn_one(lap_index, current):
        moving, collected, page_grads = current
        collected, page_grads = visit_one(moving, collected, page_grads, lap_index)
        moving = from_behind(moving, "blk", 1)
        return (moving, pass_one(collected), page_grads)

    empty_whole = jnp.zeros((bundle_size, tokens, features), jnp.float32)
    moving, collected, page_grads = lax.fori_loop(
        0, blocks - 1, turn_one, (bundle_vectors, empty_whole, page_grads)
    )
    collected, page_grads = visit_one(moving, collected, page_grads, blocks - 1)
    collected = pass_one(collected)
    grad_queries = lax.psum_scatter(collected, "group", scatter_dimension=0, tiled=True)
    return (grad_queries, page_grads, mean_loss)


def solution(mesh):
    in_specs = (
        P(("blk", "group"), None, None),
        P(("blk", "group"), None),
        P(("blk", "group")),
        P(("blk", "group"), None, None),
        P(("blk", "group"), None),
    )
    out_specs = (P(("blk", "group"), None, None), P(("blk", "group"), None, None), P())
    return jax.shard_map(
        on_device, mesh=mesh, in_specs=in_specs, out_specs=out_specs, check_vma=False
    )
```

profile of v0, /device:TPU:0, one launch (start us, length us, event | category | flops | bytes accessed | tf_op | source)
XLA Modules:
  0.0 262.9 jit_solution(15310981650806206361)
XLA Ops:
  7.2 0.8 compare_bitcast_fusion.2
  8.1 32.4 %all_gather.36 = bf16[8,16,128]{2,1,0:T(8,128)(2,1)S(1)} all-gather(bf16[1,16,128]{2,1,0:T(8,128)(2,1)S(1)} %copy-done.4), channel_id=1, replica_groups=mesh['blk'=4,'group'=8] {'group'}, dimensions={0}, use_global_device_ids=true | all-gather | bytes 36864 | tf_op jit(solution)/shard_map/all_gather | solution.py:55
  40.6 5.5 %all_gather.37 = bf16[32,16,128]{2,1,0:T(8,128)(2,1)S(1)} all-gather(bf16[8,16,128]{2,1,0:T(8,128)(2,1)S(1)} %all_gather.36), channel_id=1, replica_groups=mesh['blk'=4,'group'=8] {'blk'}, dimensions={0}, use_global_device_ids=true | all-gather | bytes 163840 | tf_op jit(solution)/shard_map/all_gather | solution.py:105
  46.8 0.7 copy-done.5
  47.5 20.4 %all-gather.2 = s32[8,1,16]{2,1,0:T(1,128)S(1)} all-gather(s32[1,1,16]{2,1,0:T(1,128)S(1)} %bitcast.182), channel_id=1, replica_groups=mesh['blk'=4,'group'=8] {'group'}, dimensions={0}, use_global_device_ids=true | all-gather | bytes 576 | tf_op jit(solution)/shard_map/all_gather | solution.py:56
  67.9 5.2 %all_gather.39 = s32[32,16]{1,0:T(8,128)S(1)} all-gather(s32[8,16]{1,0:T(8,128)S(1)} %bitcast.181), channel_id=1, replica_groups=mesh['blk'=4,'group'=8] {'blk'}, dimensions={0}, use_global_device_ids=true | all-gather | bytes 2560 | tf_op jit(solution)/shard_map/all_gather | solution.py:106
  73.1 0.7 copy-done.7
  75.0 0.8 dynamic-update-slice.28
  75.8 6.8 %all-reduce.2 = s32[8]{0:T(128)S(1)} all-reduce(s32[8]{0:T(128)S(1)} %dynamic-update-slice.28), channel_id=1, replica_groups=mesh['blk'=4,'group'=8] {'group'}, use_global_device_ids=true, to_apply=%add.2 | all-reduce | flops 8 | bytes 64
  84.1 4.9 %all-reduce.3 = s32[32]{0:T(128)S(1)} all-reduce(s32[32]{0:T(128)S(1)} %dynamic-update-slice.29), channel_id=1, replica_groups=mesh['blk'=4,'group'=8] {'blk'}, use_global_device_ids=true, to_apply=%add.3 | all-reduce | flops 32 | bytes 256
  89.2 0.7 fusion.54
  90.3 0.8 dynamic-update-slice.30
  91.0 40.5 %all-reduce.5 = (f32[1024]{0:T(1024)S(1)}, f32[1024]{0:T(1024)S(1)}, f32[32]{0:T(128)S(1)}) all-reduce(f32[1024]{0:T(1024)S(1)} %dynamic-update-slice.26, f32[1024]{0:T(1024)S(1)} %dynamic-update-slice.27, f32[32]{0:T(128)S(1)} %dynamic-update-slice.30), channel_id=2, replica_groups=mesh['blk'=4,'group'=8] {'blk','group'}, use_global_device_ids=true, to_apply=%add | all-reduce | flops 2080 | bytes 16640
  131.7 39.9 %while.48 = (s32[]{:T(128)}, f32[32]{0:T(128)S(1)}, f32[32]{0:T(128)S(1)}, f32[]{:T(128)}, f32[32,32]{1,0:T(8,128)S(1)}, /*index=5*/f32[32,32]{1,0:T(8,128)S(1)}, f32[32]{0:T(128)S(1)}, s32[]{:T(128)}, s32[]{:T(128)}, s32[]{:T(128)}) while((s32[]{:T(128)}, f32[32]{0:T(128)S(1)}, f32[32]{0:T(128)S(1)}, f32[]{:T(128)}, ...), condition=%wide.region_10.11_spmd, body=%wide.region_9.10_spmd.sunk | while | flops 198 | bytes 939 | solution.py:17
  172.6 13.9 %while.49 = (s32[]{:T(128)}, bf16[8,16,128]{2,1,0:T(8,128)(2,1)S(1)}, f32[8,16,128]{2,1,0:T(8,128)S(1)}, f32[2,128,128]{2,1,0:T(8,128)S(1)}, s32[]{:T(128)}, /*i...) while((s32[]{:T(128)}, ...), condition=%wide.region_12.13_spmd, body=%wide.region_11.12_spmd.sunk | while | flops 25395472 | bytes 1589896 | solution.py:170
  173.6 2.4 collective-permute-start.1
  176.4 0.9 collective-permute-done.1
  178.2 2.4 collective-permute-start.1
  181.0 0.9 collective-permute-done.1
  182.8 2.4 collective-permute-start.1
  185.6 0.9 collective-permute-done.1
  188.1 2.8 %collective-permute-done.2 = f32[8,16,128]{2,1,0:T(8,128)S(1)} collective-permute-done((f32[8,16,128]{2,1,0:T(8,128)S(1)}, f32[8,16,128]{2,1,0:T(8,128)S(1)}, u32[]{:S(2)}, u32[]{:S(2)}) %collective-permute-start.2) | collective-permute-done | bytes 65568 | tf_op jit(solution)/shard_map/ppermute | solution.py:25
  190.9 0.6 copy-done.2
  191.8 63.1 %reduce-scatter.2.cloned.1.call-done = f32[1,16,128]{2,1,0:T(8,128)} async-done(((f32[8,16,128]{2,1,0:T(8,128)}), f32[1,16,128]{2,1,0:T(8,128)}) %reduce-scatter.2.cloned.1.call-update) | async-done | bytes 8208 | tf_op jit(solution)/shard_map/reduce_scatter | solution.py:175
  (174 shorter events, 27.7 us)
Async XLA Ops:
  7.2 0.8 copy-start.3
  7.2 0.9 copy-start.4
  7.2 247.7 %reduce-scatter.2.cloned.1.call-start = ((), (), s32[]{:S(2)}) async-start(), calls=%async_computation.1 | async-start | bytes 73728 | tf_op jit(solution)/shard_map/reduce_scatter | solution.py:175
  40.5 5.5 %copy-start.1 = (bf16[2,128,128]{2,1,0:T(8,128)(2,1)S(1)}, bf16[2,128,128]{2,1,0:T(8,128)(2,1)}, u32[]{:S(2)}) copy-start(bf16[2,128,128]{2,1,0:T(8,128)(2,1)} %param.20) | copy-start | bytes 196612
  46.8 0.7 copy-start.5
  73.1 0.7 copy-start.7
  75.8 6.8 %copy-start.6 = (u32[32]{0:T(128)S(1)}, u32[32]{0:T(128)}, u32[]{:S(2)}) copy-start(u32[32]{0:T(128)} %constant.385) | copy-start | bytes 388
  172.6 3.7 %collective-permute-start = (bf16[8,16,128]{2,1,0:T(8,128)(2,1)S(1)}, bf16[8,16,128]{2,1,0:T(8,128)(2,1)S(1)}, u32[]{:S(2)}, u32[]{:S(2)}) collective-permute-start(bf16[8,16,128]{2,1,0:T(8,128)(2,1)S(1)} %copy.33), channel_id=1, source_target_pairs={{0,8},{8,16},{16,24},{24,0},{1,9},{9,17},{17,25},{25,1},{2,10},{10... | collective-permute-start | bytes 98312 | tf_op jit(solution)/shard_map/while/body/eval_jaxpr/ppermute | solution.py:25
  173.6 3.7 %collective-permute-start.1 = (f32[8,16,128]{2,1,0:T(8,128)S(1)}, f32[8,16,128]{2,1,0:T(8,128)S(1)}, u32[]{:S(2)}, u32[]{:S(2)}) collective-permute-start(f32[8,16,128]{2,1,0:T(8,128)S(1)} %add.305), channel_id=1, source_target_pairs={{0,8},{8,16},{16,24},{24,0},{1,9},{9,17},{17,25},{25,1},{2,10},{10... | collective-permute-start | bytes 196616 | tf_op jit(solution)/shard_map/while/body/eval_jaxpr/ppermute | solution.py:25
  177.3 3.7 %collective-permute-start = (bf16[8,16,128]{2,1,0:T(8,128)(2,1)S(1)}, bf16[8,16,128]{2,1,0:T(8,128)(2,1)S(1)}, u32[]{:S(2)}, u32[]{:S(2)}) collective-permute-start(bf16[8,16,128]{2,1,0:T(8,128)(2,1)S(1)} %copy.33), channel_id=1, source_target_pairs={{0,8},{8,16},{16,24},{24,0},{1,9},{9,17},{17,25},{25,1},{2,10},{10... | collective-permute-start | bytes 98312 | tf_op jit(solution)/shard_map/while/body/eval_jaxpr/ppermute | solution.py:25
  178.2 3.7 %collective-permute-start.1 = (f32[8,16,128]{2,1,0:T(8,128)S(1)}, f32[8,16,128]{2,1,0:T(8,128)S(1)}, u32[]{:S(2)}, u32[]{:S(2)}) collective-permute-start(f32[8,16,128]{2,1,0:T(8,128)S(1)} %add.305), channel_id=1, source_target_pairs={{0,8},{8,16},{16,24},{24,0},{1,9},{9,17},{17,25},{25,1},{2,10},{10... | collective-permute-start | bytes 196616 | tf_op jit(solution)/shard_map/while/body/eval_jaxpr/ppermute | solution.py:25
  182.0 3.6 %collective-permute-start = (bf16[8,16,128]{2,1,0:T(8,128)(2,1)S(1)}, bf16[8,16,128]{2,1,0:T(8,128)(2,1)S(1)}, u32[]{:S(2)}, u32[]{:S(2)}) collective-permute-start(bf16[8,16,128]{2,1,0:T(8,128)(2,1)S(1)} %copy.33), channel_id=1, source_target_pairs={{0,8},{8,16},{16,24},{24,0},{1,9},{9,17},{17,25},{25,1},{2,10},{10... | collective-permute-start | bytes 98312 | tf_op jit(solution)/shard_map/while/body/eval_jaxpr/ppermute | solution.py:25
  182.8 3.7 %collective-permute-start.1 = (f32[8,16,128]{2,1,0:T(8,128)S(1)}, f32[8,16,128]{2,1,0:T(8,128)S(1)}, u32[]{:S(2)}, u32[]{:S(2)}) collective-permute-start(f32[8,16,128]{2,1,0:T(8,128)S(1)} %add.305), channel_id=1, source_target_pairs={{0,8},{8,16},{16,24},{24,0},{1,9},{9,17},{17,25},{25,1},{2,10},{10... | collective-permute-start | bytes 196616 | tf_op jit(solution)/shard_map/while/body/eval_jaxpr/ppermute | solution.py:25
  187.2 3.7 %collective-permute-start.2 = (f32[8,16,128]{2,1,0:T(8,128)S(1)}, f32[8,16,128]{2,1,0:T(8,128)S(1)}, u32[]{:S(2)}, u32[]{:S(2)}) collective-permute-start(f32[8,16,128]{2,1,0:T(8,128)S(1)} %add.250), channel_id=1, source_target_pairs={{0,8},{8,16},{16,24},{24,0},{1,9},{9,17},{17,25},{25,1},{2,10},{10... | collective-permute-start | bytes 196616 | tf_op jit(solution)/shard_map/ppermute | solution.py:25
  190.9 0.6 copy-start.2
  191.8 63.1 %copy-start = (f32[2,128,128]{2,1,0:T(8,128)}, f32[2,128,128]{2,1,0:T(8,128)S(1)}, u32[]{:S(2)}) copy-start(f32[2,128,128]{2,1,0:T(8,128)S(1)} %fusion.38) | copy-start | bytes 393220
Sparse Core Ops, SparseCore 0:
  191.7 63.1 reduce-scatter.1
where the time goes:
time: 264 us; the launch traced here: 263 us
  blocking collectives  116 us (44%)
  waiting for transfers between devices  68.8 us (26%)
  local copies, waits for them, and re-layouts  24.5 us (9%)
  loops' own time  21.1 us (8%)
  between operations  17.3 us (7%)
  starting transfers between devices  7.44 us (3%)
  matrix products  4.3 us (2%)
  other arithmetic  3.58 us (1%)
    reduce_scatter x1, waiting for transfers between devices, on_device(): lax.psum_scatter(collected, 'group', scatter_dimension=0, tiled=True)  63.1 us
    unnamed x3, blocking collectives  52.2 us
    all_gather x1, blocking collectives, on_device(): lax.all_gather(queries, 'group', axis=0, tiled=True)  32.4 us
    another operation x1, loops' own time, combined_all(): lax.fori_loop(1, lax.axis_size(axis), lambda source, state: combine(state...  20.9 us
    all_gather x1, blocking collectives, on_device(): lax.all_gather(query_mask, 'group', axis=0, tiled=True)  20.4 us
    dynamic_slice x33, local copies, waits for them, and re-layouts, take(): lax.dynamic_index_in_dim(a, source, 0, False)  18.2 us
    ppermute x7, starting transfers between devices, from_behind(): return lax.ppermute(value, axis, pairs)  7.4 us
    ppermute x7, waiting for transfers between devices, from_behind(): return lax.ppermute(value, axis, pairs)  5.66 us
  transfers between devices with their start and end apart: 8, of which 5 were waited for; matrix products, arithmetic and copies ran while one was open for 1% of the time, Pallas kernels for 0%

commit v1 on v0

--- a/solution.py
+++ b/solution.py
@@ -6,6 +6,17 @@
 
 relaxation_scale_factor = 0.5
 guarded_floor_entry = -1e30
+
+
+def ring_gather(x, axis, dim):
+    ways = lax.axis_size(axis)
+    pieces = [x]
+    for far in range(1, ways):
+        pieces.append(
+            lax.ppermute(pieces[far - 1], axis, [(d, (d - 1) % ways) for d in range(ways)])
+        )
+    line = jnp.concatenate(pieces, axis=dim)
+    return jnp.roll(line, lax.axis_index(axis) * x.shape[dim], axis=dim)
 
 
 def combined_all(part, axis, combine):
@@ -53,7 +64,7 @@
     natural_logarithm_lengths = jnp.log(jnp.sum(page_mask.astype(jnp.float32), axis=1))
     bundle_vectors, bundle_masks, bundle_targets = (
         lax.all_gather(queries, "group", axis=0, tiled=True),
-        lax.all_gather(query_mask, "group", axis=0, tiled=True),
+        ring_gather(query_mask, "group", 0),
         lax.all_gather(positive, "group", axis=0, tiled=True),
     )
 

time: 264 us -> 285 us (1.080)
  starting transfers between devices: 7.44 us -> 41.1 us
  blocking collectives: 116 us -> 94.6 us
  waiting for transfers between devices: 68.8 us -> 76.9 us
    ppermute x0 -> x7, starting transfers between devices: none -> 33.7 us  [ring_gather(): lax.ppermute(pieces[far - 1], axis, [(d, (d - 1) % ways) for d in range(w...]
    all_gather x1 -> x0, blocking collectives: 20.4 us -> none  [on_device(): lax.all_gather(query_mask, 'group', axis=0, tiled=True)]
    ppermute x0 -> x7, waiting for transfers between devices: none -> 7.77 us  [ring_gather(): lax.ppermute(pieces[far - 1], axis, [(d, (d - 1) % ways) for d in range(w...]
  transfers between devices with their start and end apart: 8 -> 15, of which waited for: 5 -> 11; matrix products, arithmetic and copies ran while one was open for 1% -> 3% of each run, Pallas kernels for 0% -> 0%
where the time goes in v1:
time: 285 us; the launch traced here: 284 us
  blocking collectives  94.6 us (33%)
  waiting for transfers between devices  76.9 us (27%)
  starting transfers between devices  41.1 us (14%)
  local copies, waits for them, and re-layouts  25.5 us (9%)
  loops' own time  21.1 us (7%)
  between operations  17.4 us (6%)
  matrix products  4.31 us (2%)
  other arithmetic  2.96 us (1%)
    reduce_scatter x1, waiting for transfers between devices, on_device(): lax.psum_scatter(collected, 'group', scatter_dimension=0, tiled=True)  63.4 us
    unnamed x3, blocking collectives  53.3 us
    ppermute x7, starting transfers between devices, ring_gather(): lax.ppermute(pieces[far - 1], axis, [(d, (d - 1) % ways) for d in range(w...  33.7 us
    all_gather x1, blocking collectives, on_device(): lax.all_gather(queries, 'group', axis=0, tiled=True)  30.6 us
    another operation x1, loops' own time, combined_all(): lax.fori_loop(1, lax.axis_size(axis), lambda source, state: combine(state...  20.9 us
    dynamic_slice x33, local copies, waits for them, and re-layouts, take(): lax.dynamic_index_in_dim(a, source, 0, False)  18.2 us
    ppermute x7, waiting for transfers between devices, ring_gather(): lax.ppermute(pieces[far - 1], axis, [(d, (d - 1) % ways) for d in range(w...  7.77 us
    ppermute x7, starting transfers between devices, from_behind(): return lax.ppermute(value, axis, pairs)  7.4 us
  transfers between devices with their start and end apart: 15, of which 11 were waited for; matrix products, arithmetic and copies ran while one was open for 3% of the time, Pallas kernels for 0%

profile of v1, /device:TPU:0, one launch (start us, length us, event | category | flops | bytes accessed | tf_op | source)
XLA Modules:
  0.0 283.9 jit_solution(11900771965082065390)
XLA Ops:
  7.2 6.1 %collective-permute-start.2 = (s32[1,16]{1,0:T(1,128)}, s32[1,16]{1,0:T(1,128)S(1)}, u32[]{:S(2)}, u32[]{:S(2)}) collective-permute-start(s32[1,16]{1,0:T(1,128)} %param.18), channel_id=1, source_target_pairs={{0,7},{1,0},{2,1},{3,2},{4,3},{5,4},{6,5},{7,6},{8,15},{9,8},{10,9... | collective-permute-start | bytes 200 | tf_op jit(solution)/shard_map/ppermute | solution.py:16
  14.8 30.6 %all_gather.33 = bf16[8,16,128]{2,1,0:T(8,128)(2,1)S(1)} all-gather(bf16[1,16,128]{2,1,0:T(8,128)(2,1)S(1)} %copy-done.4), channel_id=1, replica_groups=mesh['blk'=4,'group'=8] {'group'}, dimensions={0}, use_global_device_ids=true | all-gather | bytes 36864 | tf_op jit(solution)/shard_map/all_gather | solution.py:66
  45.4 5.5 %all_gather.34 = bf16[32,16,128]{2,1,0:T(8,128)(2,1)S(1)} all-gather(bf16[8,16,128]{2,1,0:T(8,128)(2,1)S(1)} %all_gather.33), channel_id=1, replica_groups=mesh['blk'=4,'group'=8] {'blk'}, dimensions={0}, use_global_device_ids=true | all-gather | bytes 163840 | tf_op jit(solution)/shard_map/all_gather | solution.py:116
  54.5 8.6 %all-reduce.2 = s32[8]{0:T(128)S(1)} all-reduce(s32[8]{0:T(128)S(1)} %dynamic-update-slice.28), channel_id=1, replica_groups=mesh['blk'=4,'group'=8] {'group'}, use_global_device_ids=true, to_apply=%add.2 | all-reduce | flops 8 | bytes 64
  64.7 4.9 %all-reduce.3 = s32[32]{0:T(128)S(1)} all-reduce(s32[32]{0:T(128)S(1)} %dynamic-update-slice.29), channel_id=1, replica_groups=mesh['blk'=4,'group'=8] {'blk'}, use_global_device_ids=true, to_apply=%add.3 | all-reduce | flops 32 | bytes 256
  69.6 2.8 collective-permute-start.3
  72.4 1.3 collective-permute-done.3
  73.7 5.0 %collective-permute-start.4 = (s32[1,16]{1,0:T(1,128)S(1)}, s32[1,16]{1,0:T(1,128)S(1)}, u32[]{:S(2)}, u32[]{:S(2)}) collective-permute-start(s32[1,16]{1,0:T(1,128)S(1)} %collective-permute-done.3), channel_id=1, source_target_pairs={{0,7},{1,0},{2,1},{3,2},{4,3},{5,4},{6,5},{7,6},{8,15},{9,8},{10,9... | collective-permute-start | bytes 200 | tf_op jit(solution)/shard_map/ppermute | solution.py:16
  78.7 1.3 collective-permute-done.4
  79.9 5.0 %collective-permute-start.5 = (s32[1,16]{1,0:T(1,128)S(1)}, s32[1,16]{1,0:T(1,128)S(1)}, u32[]{:S(2)}, u32[]{:S(2)}) collective-permute-start(s32[1,16]{1,0:T(1,128)S(1)} %collective-permute-done.4), channel_id=1, source_target_pairs={{0,7},{1,0},{2,1},{3,2},{4,3},{5,4},{6,5},{7,6},{8,15},{9,8},{10,9... | collective-permute-start | bytes 200 | tf_op jit(solution)/shard_map/ppermute | solution.py:16
  84.9 1.3 collective-permute-done.5
  86.2 5.0 %collective-permute-start.6 = (s32[1,16]{1,0:T(1,128)S(1)}, s32[1,16]{1,0:T(1,128)S(1)}, u32[]{:S(2)}, u32[]{:S(2)}) collective-permute-start(s32[1,16]{1,0:T(1,128)S(1)} %collective-permute-done.5), channel_id=1, source_target_pairs={{0,7},{1,0},{2,1},{3,2},{4,3},{5,4},{6,5},{7,6},{8,15},{9,8},{10,9... | collective-permute-start | bytes 200 | tf_op jit(solution)/shard_map/ppermute | solution.py:16
  91.2 1.3 collective-permute-done.6
  92.5 5.0 %collective-permute-start.7 = (s32[1,16]{1,0:T(1,128)S(1)}, s32[1,16]{1,0:T(1,128)S(1)}, u32[]{:S(2)}, u32[]{:S(2)}) collective-permute-start(s32[1,16]{1,0:T(1,128)S(1)} %collective-permute-done.6), channel_id=1, source_target_pairs={{0,7},{1,0},{2,1},{3,2},{4,3},{5,4},{6,5},{7,6},{8,15},{9,8},{10,9... | collective-permute-start | bytes 200 | tf_op jit(solution)/shard_map/ppermute | solution.py:16
  98.7 5.0 %collective-permute-start.8 = (s32[1,16]{1,0:T(1,128)S(1)}, s32[1,16]{1,0:T(1,128)S(1)}, u32[]{:S(2)}, u32[]{:S(2)}) collective-permute-start(s32[1,16]{1,0:T(1,128)S(1)} %collective-permute-done.7), channel_id=1, source_target_pairs={{0,7},{1,0},{2,1},{3,2},{4,3},{5,4},{6,5},{7,6},{8,15},{9,8},{10,9... | collective-permute-start | bytes 200 | tf_op jit(solution)/shard_map/ppermute | solution.py:16
  105.1 5.2 %all_gather.35 = s32[32,16]{1,0:T(8,128)S(1)} all-gather(s32[8,16]{1,0:T(8,128)S(1)} %constant_dynamic-slice_fusion.5), channel_id=1, replica_groups=mesh['blk'=4,'group'=8] {'blk'}, dimensions={0}, use_global_device_ids=true | all-gather | bytes 2560 | tf_op jit(solution)/shard_map/all_gather | solution.py:117
  112.4 39.8 %all-reduce.5 = (f32[1024]{0:T(1024)S(1)}, f32[1024]{0:T(1024)S(1)}, f32[32]{0:T(128)S(1)}) all-reduce(f32[1024]{0:T(1024)S(1)} %dynamic-update-slice.26, f32[1024]{0:T(1024)S(1)} %dynamic-update-slice.27, f32[32]{0:T(128)S(1)} %dynamic-update-slice.30), channel_id=2, replica_groups=mesh['blk'=4,'group'=8] {'blk','group'}, use_global_device_ids=true, to_apply=%add | all-reduce | flops 2080 | bytes 16640
  152.4 40.0 %while.48 = (s32[]{:T(128)}, f32[32]{0:T(128)S(1)}, f32[32]{0:T(128)S(1)}, f32[]{:T(128)}, f32[32,32]{1,0:T(8,128)S(1)}, /*index=5*/f32[32,32]{1,0:T(8,128)S(1)}, f32[32]{0:T(128)S(1)}, s32[]{:T(128)}, s32[]{:T(128)}, s32[]{:T(128)}) while((s32[]{:T(128)}, f32[32]{0:T(128)S(1)}, f32[32]{0:T(128)S(1)}, f32[]{:T(128)}, ...), condition=%wide.region_10.11_spmd, body=%wide.region_9.10_spmd.sunk | while | flops 198 | bytes 939 | solution.py:28
  193.4 13.9 %while.49 = (s32[]{:T(128)}, bf16[8,16,128]{2,1,0:T(8,128)(2,1)S(1)}, f32[8,16,128]{2,1,0:T(8,128)S(1)}, f32[2,128,128]{2,1,0:T(8,128)S(1)}, s32[]{:T(128)}, /*i...) while((s32[]{:T(128)}, ...), condition=%wide.region_12.13_spmd, body=%wide.region_11.12_spmd.sunk | while | flops 25395472 | bytes 1589896 | solution.py:181
  194.3 2.4 collective-permute-start.1
  199.0 2.4 collective-permute-start.1
  203.6 2.4 collective-permute-start.1
  208.9 2.8 collective-permute-done.9
  212.5 63.4 %reduce-scatter.2.cloned.1.call-done = f32[1,16,128]{2,1,0:T(8,128)} async-done(((f32[8,16,128]{2,1,0:T(8,128)}), f32[1,16,128]{2,1,0:T(8,128)}) %reduce-scatter.2.cloned.1.call-update) | async-done | bytes 8208 | tf_op jit(solution)/shard_map/reduce_scatter | solution.py:186
  (189 shorter events, 38.4 us)
Async XLA Ops:
  7.2 268.8 %reduce-scatter.2.cloned.1.call-start = ((), (), s32[]{:S(2)}) async-start(), calls=%async_computation.1 | async-start | bytes 73728 | tf_op jit(solution)/shard_map/reduce_scatter | solution.py:186
  7.2 62.4 %collective-permute-start.2 = (s32[1,16]{1,0:T(1,128)}, s32[1,16]{1,0:T(1,128)S(1)}, u32[]{:S(2)}, u32[]{:S(2)}) collective-permute-start(s32[1,16]{1,0:T(1,128)} %param.18), channel_id=1, source_target_pairs={{0,7},{1,0},{2,1},{3,2},{4,3},{5,4},{6,5},{7,6},{8,15},{9,8},{10,9... | collective-permute-start | bytes 200 | tf_op jit(solution)/shard_map/ppermute | solution.py:16
  13.3 0.7 copy-start.3
  14.1 0.7 copy-start.4
  45.4 5.5 %copy-start.1 = (bf16[2,128,128]{2,1,0:T(8,128)(2,1)S(1)}, bf16[2,128,128]{2,1,0:T(8,128)(2,1)}, u32[]{:S(2)}) copy-start(bf16[2,128,128]{2,1,0:T(8,128)(2,1)} %param.20) | copy-start | bytes 196612
  51.7 0.7 copy-start.7
  54.5 8.6 %copy-start.6 = (u32[32]{0:T(128)S(1)}, u32[32]{0:T(128)}, u32[]{:S(2)}) copy-start(u32[32]{0:T(128)} %constant.405) | copy-start | bytes 388
  69.6 4.1 %collective-permute-start.3 = (s32[1,16]{1,0:T(1,128)S(1)}, s32[1,16]{1,0:T(1,128)S(1)}, u32[]{:S(2)}, u32[]{:S(2)}) collective-permute-start(s32[1,16]{1,0:T(1,128)S(1)} %collective-permute-done.2), channel_id=1, source_target_pairs={{0,7},{1,0},{2,1},{3,2},{4,3},{5,4},{6,5},{7,6},{8,15},{9,8},{10,9... | collective-permute-start | bytes 200 | tf_op jit(solution)/shard_map/ppermute | solution.py:16
  73.7 6.3 %collective-permute-start.4 = (s32[1,16]{1,0:T(1,128)S(1)}, s32[1,16]{1,0:T(1,128)S(1)}, u32[]{:S(2)}, u32[]{:S(2)}) collective-permute-start(s32[1,16]{1,0:T(1,128)S(1)} %collective-permute-done.3), channel_id=1, source_target_pairs={{0,7},{1,0},{2,1},{3,2},{4,3},{5,4},{6,5},{7,6},{8,15},{9,8},{10,9... | collective-permute-start | bytes 200 | tf_op jit(solution)/shard_map/ppermute | solution.py:16
  79.9 6.3 %collective-permute-start.5 = (s32[1,16]{1,0:T(1,128)S(1)}, s32[1,16]{1,0:T(1,128)S(1)}, u32[]{:S(2)}, u32[]{:S(2)}) collective-permute-start(s32[1,16]{1,0:T(1,128)S(1)} %collective-permute-done.4), channel_id=1, source_target_pairs={{0,7},{1,0},{2,1},{3,2},{4,3},{5,4},{6,5},{7,6},{8,15},{9,8},{10,9... | collective-permute-start | bytes 200 | tf_op jit(solution)/shard_map/ppermute | solution.py:16
  86.2 6.3 %collective-permute-start.6 = (s32[1,16]{1,0:T(1,128)S(1)}, s32[1,16]{1,0:T(1,128)S(1)}, u32[]{:S(2)}, u32[]{:S(2)}) collective-permute-start(s32[1,16]{1,0:T(1,128)S(1)} %collective-permute-done.5), channel_id=1, source_target_pairs={{0,7},{1,0},{2,1},{3,2},{4,3},{5,4},{6,5},{7,6},{8,15},{9,8},{10,9... | collective-permute-start | bytes 200 | tf_op jit(solution)/shard_map/ppermute | solution.py:16
  92.5 6.3 %collective-permute-start.7 = (s32[1,16]{1,0:T(1,128)S(1)}, s32[1,16]{1,0:T(1,128)S(1)}, u32[]{:S(2)}, u32[]{:S(2)}) collective-permute-start(s32[1,16]{1,0:T(1,128)S(1)} %collective-permute-done.6), channel_id=1, source_target_pairs={{0,7},{1,0},{2,1},{3,2},{4,3},{5,4},{6,5},{7,6},{8,15},{9,8},{10,9... | collective-permute-start | bytes 200 | tf_op jit(solution)/shard_map/ppermute | solution.py:16
  97.5 7.6 %copy-start.5 = (s32[1,16]{1,0:T(1,128)S(1)}, s32[1,16]{1,0:T(1,128)}, u32[]{:S(2)}) copy-start(s32[1,16]{1,0:T(1,128)} %param.18) | copy-start | bytes 196
  98.7 6.3 %collective-permute-start.8 = (s32[1,16]{1,0:T(1,128)S(1)}, s32[1,16]{1,0:T(1,128)S(1)}, u32[]{:S(2)}, u32[]{:S(2)}) collective-permute-start(s32[1,16]{1,0:T(1,128)S(1)} %collective-permute-done.7), channel_id=1, source_target_pairs={{0,7},{1,0},{2,1},{3,2},{4,3},{5,4},{6,5},{7,6},{8,15},{9,8},{10,9... | collective-permute-start | bytes 200 | tf_op jit(solution)/shard_map/ppermute | solution.py:16
  193.4 3.7 %collective-permute-start = (bf16[8,16,128]{2,1,0:T(8,128)(2,1)S(1)}, bf16[8,16,128]{2,1,0:T(8,128)(2,1)S(1)}, u32[]{:S(2)}, u32[]{:S(2)}) collective-permute-start(bf16[8,16,128]{2,1,0:T(8,128)(2,1)S(1)} %copy.33), channel_id=1, source_target_pairs={{0,8},{8,16},{16,24},{24,0},{1,9},{9,17},{17,25},{25,1},{2,10},{10... | collective-permute-start | bytes 98312 | tf_op jit(solution)/shard_map/while/body/eval_jaxpr/ppermute | solution.py:36
  194.3 3.7 %collective-permute-start.1 = (f32[8,16,128]{2,1,0:T(8,128)S(1)}, f32[8,16,128]{2,1,0:T(8,128)S(1)}, u32[]{:S(2)}, u32[]{:S(2)}) collective-permute-start(f32[8,16,128]{2,1,0:T(8,128)S(1)} %add.317), channel_id=1, source_target_pairs={{0,8},{8,16},{16,24},{24,0},{1,9},{9,17},{17,25},{25,1},{2,10},{10... | collective-permute-start | bytes 196616 | tf_op jit(solution)/shard_map/while/body/eval_jaxpr/ppermute | solution.py:36
  198.1 3.7 %collective-permute-start = (bf16[8,16,128]{2,1,0:T(8,128)(2,1)S(1)}, bf16[8,16,128]{2,1,0:T(8,128)(2,1)S(1)}, u32[]{:S(2)}, u32[]{:S(2)}) collective-permute-start(bf16[8,16,128]{2,1,0:T(8,128)(2,1)S(1)} %copy.33), channel_id=1, source_target_pairs={{0,8},{8,16},{16,24},{24,0},{1,9},{9,17},{17,25},{25,1},{2,10},{10... | collective-permute-start | bytes 98312 | tf_op jit(solution)/shard_map/while/body/eval_jaxpr/ppermute | solution.py:36
  199.0 3.7 %collective-permute-start.1 = (f32[8,16,128]{2,1,0:T(8,128)S(1)}, f32[8,16,128]{2,1,0:T(8,128)S(1)}, u32[]{:S(2)}, u32[]{:S(2)}) collective-permute-start(f32[8,16,128]{2,1,0:T(8,128)S(1)} %add.317), channel_id=1, source_target_pairs={{0,8},{8,16},{16,24},{24,0},{1,9},{9,17},{17,25},{25,1},{2,10},{10... | collective-permute-start | bytes 196616 | tf_op jit(solution)/shard_map/while/body/eval_jaxpr/ppermute | solution.py:36
  202.7 3.6 %collective-permute-start = (bf16[8,16,128]{2,1,0:T(8,128)(2,1)S(1)}, bf16[8,16,128]{2,1,0:T(8,128)(2,1)S(1)}, u32[]{:S(2)}, u32[]{:S(2)}) collective-permute-start(bf16[8,16,128]{2,1,0:T(8,128)(2,1)S(1)} %copy.33), channel_id=1, source_target_pairs={{0,8},{8,16},{16,24},{24,0},{1,9},{9,17},{17,25},{25,1},{2,10},{10... | collective-permute-start | bytes 98312 | tf_op jit(solution)/shard_map/while/body/eval_jaxpr/ppermute | solution.py:36
  203.6 3.7 %collective-permute-start.1 = (f32[8,16,128]{2,1,0:T(8,128)S(1)}, f32[8,16,128]{2,1,0:T(8,128)S(1)}, u32[]{:S(2)}, u32[]{:S(2)}) collective-permute-start(f32[8,16,128]{2,1,0:T(8,128)S(1)} %add.317), channel_id=1, source_target_pairs={{0,8},{8,16},{16,24},{24,0},{1,9},{9,17},{17,25},{25,1},{2,10},{10... | collective-permute-start | bytes 196616 | tf_op jit(solution)/shard_map/while/body/eval_jaxpr/ppermute | solution.py:36
  208.0 3.7 %collective-permute-start.9 = (f32[8,16,128]{2,1,0:T(8,128)S(1)}, f32[8,16,128]{2,1,0:T(8,128)S(1)}, u32[]{:S(2)}, u32[]{:S(2)}) collective-permute-start(f32[8,16,128]{2,1,0:T(8,128)S(1)} %add.262), channel_id=1, source_target_pairs={{0,8},{8,16},{16,24},{24,0},{1,9},{9,17},{17,25},{25,1},{2,10},{10... | collective-permute-start | bytes 196616 | tf_op jit(solution)/shard_map/ppermute | solution.py:36
  211.7 0.6 copy-start.2
  212.5 63.4 %copy-start = (f32[2,128,128]{2,1,0:T(8,128)}, f32[2,128,128]{2,1,0:T(8,128)S(1)}, u32[]{:S(2)}) copy-start(f32[2,128,128]{2,1,0:T(8,128)S(1)} %fusion.38) | copy-start | bytes 393220
Sparse Core Ops, SparseCore 0:
  212.5 63.4 reduce-scatter.1
